TPU v7x, 32 devices: a whole 2x2x4 slice. The times are simulated.
32 devices in a mesh: dp: 4 (over z), graph: 8 (over y, x, core).
Axes of the slice: x: 2, y: 2, z: 4, core: 2. Of those that a mesh axis runs over, the one named last changes fastest.
Arguments:
- features: float32 [4, 128, 3200], P('dp', 'graph'), may hold values from -6 to 6
- cotangent: float32 [4, 128, 1600], P('dp', 'graph'), may hold values from -6 to 6
- rotation: bfloat16 [4, 114, 1536], P('dp', None, 'graph'), may hold values from -2.6875 to 2.6875
- send_left: int32 [4, 64], P('dp', 'graph'), may hold values from 0 to 16, as said below
- send_right: int32 [4, 64], P('dp', 'graph'), may hold values from 0 to 16, as said below
- edge_src: int32 [4, 1536], P('dp', 'graph'), may hold values from 0 to 31, as said below
- edge_tgt: int32 [4, 1536], P('dp', 'graph'), may hold values from 0 to 15, as said below
- w_zero: bfloat16 [640, 832], P('graph'), may hold values from -0.25 to 0.25
- w_one_re: bfloat16 [512, 256], P('graph'), may hold values from -0.1875 to 0.1875
- w_one_im: bfloat16 [512, 256], P('graph'), may hold values from -0.1875 to 0.1875
- w_two_re: bfloat16 [384, 192], P('graph'), may hold values from -0.21875 to 0.21875
- w_two_im: bfloat16 [384, 192], P('graph'), may hold values from -0.21875 to 0.21875
- w_target: bfloat16 [128, 512], P('graph'), may hold values from -0.5 to 0.5
- alpha_vec: bfloat16 [64, 8], P('graph'), may hold values from -0.75 to 0.75
Outputs:
- attended: bfloat16 [4, 128, 1600], P('dp', 'graph')
- grad_features: float32 [4, 128, 3200], P('dp', 'graph')
- grad_zero: float32 [640, 832], P('graph')
- grad_one_re: float32 [512, 256], P('graph')
- grad_one_im: float32 [512, 256], P('graph')
- grad_two_re: float32 [384, 192], P('graph')
- grad_two_im: float32 [384, 192], P('graph')
- grad_target: float32 [128, 512], P('graph')
- grad_alpha: float32 [64, 8], P('graph')
Inputs may be any that keep to these rules, and one draw needn't show every extreme that they name: `send_left`: filled slots come first and name distinct atoms; the value 16 marks an empty slot; each list holds 4 or more atoms, and in every cell some slab fills all 8 slots. `send_right`: like send_left. `edge_src`: values below 16 are the slab's own atoms; 16 + k is slot k of slab g-1's send_right, 24 + k slot k of slab g+1's send_left; never an empty slot. `edge_tgt`: every atom of a slab is the target of one edge or more.
All inputs are finite; a program needn't handle non-finite values.
Results may differ from a plain program's by a relative error of at most 0.0085.
Values may be sent and summed in bfloat16 or wider, within the bound.
A program may use at most 128 MiB of HBM per device.

v0:
```python
from functools import partial
import jax
import jax.numpy as jnp
from jax import lax
from jax.sharding import PartitionSpec as P


def padded_2(block, sides, width):
    for axis, dim in sides:
        count = lax.axis_size(axis)
        forward = [(i, i + 1) for i in range(count - 1)]
        forward.append((count - 1, 0))
        backward = [(target, source) for source, target in forward]
        low = lax.ppermute(
            lax.slice_in_dim(block, block.shape[dim] - width, None, axis=dim), axis, forward
        )
        high = lax.ppermute(lax.slice_in_dim(block, 0, width, axis=dim), axis, backward)
        block = jnp.concatenate([low, block, high], axis=dim)
    return block


def turn_blocks(rotation, edge_count):
    blocks = []
    offset = 0
    for degree in range(1, 5):
        kept_order = min(degree, 2)
        row_count = 2 * kept_order + 1
        column_count = 2 * degree + 1
        piece_block = rotation[offset : offset + row_count * column_count].astype(jnp.float32)
        blocks.append(piece_block.reshape(row_count, column_count, edge_count))
        offset = offset + row_count * column_count
    return blocks


def apply_block(block, source_part):
    rows_out = []
    for row in range(block.shape[0]):
        total = block[row, 0][:, None] * source_part[:, 0, :]
        for column in range(1, block.shape[1]):
            total = total + block[row, column][:, None] * source_part[:, column, :]
        rows_out.append(total)
    return jnp.stack(rows_out, axis=1)


def apply_back(block, stacked):
    columns_out = []
    for column in range(block.shape[1]):
        total = block[0, column][:, None] * stacked[:, 0, :]
        for row in range(1, block.shape[0]):
            total = total + block[row, column][:, None] * stacked[:, row, :]
        columns_out.append(total)
    return jnp.stack(columns_out, axis=1)


def pick_order(turned, azimuth, degrees, edge_count):
    chosen = jnp.stack(
        [turned[degree][:, min(degree, 2) + azimuth, :] for degree in degrees], axis=1
    )
    return chosen.reshape(edge_count, -1).astype(jnp.bfloat16)


def attend(
    extended,
    w_zero,
    w_one_re,
    w_one_im,
    w_two_re,
    w_two_im,
    w_target,
    alpha_vec,
    rotation,
    edge_src,
    edge_tgt,
    atom_count,
):
    edge_count = edge_src.shape[0]
    channels = w_target.shape[0]
    hidden = w_one_re.shape[1] // 4
    head_count = alpha_vec.shape[1]
    alpha_width = alpha_vec.shape[0]
    blocks = turn_blocks(rotation, edge_count)
    coeffs = extended.reshape(extended.shape[0], 25, channels)
    turned = [jnp.take(coeffs[:, 0:1, :], edge_src, axis=0)]
    for degree in range(1, 5):
        source_part = jnp.take(
            coeffs[:, degree * degree : (degree + 1) * (degree + 1), :], edge_src, axis=0
        )
        turned.append(apply_block(blocks[degree - 1], source_part))
    zero_in = pick_order(turned, 0, range(5), edge_count)
    one_pos = pick_order(turned, 1, range(1, 5), edge_count)
    one_neg = pick_order(turned, -1, range(1, 5), edge_count)
    two_pos = pick_order(turned, 2, range(2, 5), edge_count)
    two_neg = pick_order(turned, -2, range(2, 5), edge_count)
    mixed = jnp.dot(zero_in, w_zero, preferred_element_type=jnp.float32)
    hidden_zero = mixed[:, : 5 * hidden].reshape(edge_count, 5, hidden)
    target_in = extended[:atom_count, :channels].astype(jnp.bfloat16)
    per_atom = jnp.dot(target_in, w_target, preferred_element_type=jnp.float32)
    alpha_pre = mixed[:, 5 * hidden :] + jnp.take(per_atom, edge_tgt, axis=0)
    one_up = jnp.dot(one_pos, w_one_re, preferred_element_type=jnp.float32) - jnp.dot(
        one_neg, w_one_im, preferred_element_type=jnp.float32
    )
    one_down = jnp.dot(one_neg, w_one_re, preferred_element_type=jnp.float32) + jnp.dot(
        one_pos, w_one_im, preferred_element_type=jnp.float32
    )
    two_up = jnp.dot(two_pos, w_two_re, preferred_element_type=jnp.float32) - jnp.dot(
        two_neg, w_two_im, preferred_element_type=jnp.float32
    )
    two_down = jnp.dot(two_neg, w_two_re, preferred_element_type=jnp.float32) + jnp.dot(
        two_pos, w_two_im, preferred_element_type=jnp.float32
    )
    scalar = hidden_zero[:, 0, :]
    gating = jax.nn.sigmoid(scalar)[:, None, :]
    value_zero = jnp.concatenate(
        [jax.nn.silu(scalar)[:, None, :], hidden_zero[:, 1:, :] * gating], axis=1
    )
    one_up = one_up.reshape(edge_count, 4, hidden) * gating
    one_down = one_down.reshape(edge_count, 4, hidden) * gating
    two_up = two_up.reshape(edge_count, 3, hidden) * gating
    two_down = two_down.reshape(edge_count, 3, hidden) * gating
    scores = alpha_pre.reshape(edge_count, head_count, alpha_width)
    centre = scores - jnp.mean(scores, axis=-1, keepdims=True)
    normed = centre * lax.rsqrt(jnp.mean(centre * centre, axis=-1, keepdims=True) + 1e-05)
    activated = normed * (0.2 + 0.8 * jax.nn.sigmoid(normed))
    logits = jnp.einsum(
        "ehc,ch->eh", activated, alpha_vec.astype(jnp.float32), precision=lax.Precision.HIGHEST
    )
    raised = jnp.exp(logits)
    member = (edge_tgt[:, None] == jnp.arange(atom_count, dtype=jnp.int32)[None, :]).astype(
        jnp.float32
    )
    totals = jnp.dot(member.T, raised, precision=lax.Precision.HIGHEST)
    weights = raised / jnp.take(totals, edge_tgt, axis=0)
    spread = jnp.repeat(weights, hidden // head_count, axis=1)[:, None, :]
    value_zero = value_zero * spread
    one_up = one_up * spread
    one_down = one_down * spread
    two_up = two_up * spread
    two_down = two_down * spread
    pieces = [value_zero[:, 0:1, :]]
    for degree in range(1, 5):
        kept_order = min(degree, 2)
        row_list = []
        for azimuth in range(-kept_order, kept_order + 1):
            if azimuth == 0:
                row_list.append(value_zero[:, degree])
            elif azimuth == 1:
                row_list.append(one_up[:, degree - 1])
            elif azimuth == -1:
                row_list.append(one_down[:, degree - 1])
            elif azimuth == 2:
                row_list.append(two_up[:, degree - 2])
            else:
                row_list.append(two_down[:, degree - 2])
        stacked = jnp.stack(row_list, axis=1)
        pieces.append(apply_back(blocks[degree - 1], stacked))
    message = jnp.concatenate(pieces, axis=1).reshape(edge_count, -1).astype(jnp.bfloat16)
    return jnp.dot(member.T.astype(jnp.bfloat16), message, preferred_element_type=jnp.float32)


def body(
    features,
    cotangent,
    rotation,
    send_left,
    send_right,
    edge_src,
    edge_tgt,
    w_zero,
    w_one_re,
    w_one_im,
    w_two_re,
    w_two_im,
    w_target,
    alpha_vec,
):
    full_weights = (
        lax.all_gather(w_zero, "graph", axis=0, tiled=True),
        lax.all_gather(w_one_re, "graph", axis=0, tiled=True),
        lax.all_gather(w_one_im, "graph", axis=0, tiled=True),
        lax.all_gather(w_two_re, "graph", axis=0, tiled=True),
        lax.all_gather(w_two_im, "graph", axis=0, tiled=True),
        lax.all_gather(w_target, "graph", axis=0, tiled=True),
        lax.all_gather(alpha_vec, "graph", axis=0, tiled=True),
    )
    own_rows = features[0]
    atom_count = own_rows.shape[0]
    ghost_count = send_left.shape[1]
    row_width = own_rows.shape[1]
    padded = jnp.concatenate([own_rows, jnp.zeros((1, row_width), jnp.float32)], axis=0)
    outgoing = jnp.concatenate(
        [jnp.take(padded, send_left[0], axis=0), jnp.take(padded, send_right[0], axis=0)], axis=0
    )
    widened = padded_2(outgoing, (("graph", 0),), ghost_count)
    extended = jnp.concatenate(
        [own_rows, widened[:ghost_count], widened[3 * ghost_count :]], axis=0
    )
    local_fn = partial(
        attend,
        rotation=rotation[0],
        edge_src=edge_src[0],
        edge_tgt=edge_tgt[0],
        atom_count=atom_count,
    )
    summed, pullback = jax.vjp(
        local_fn,
        extended,
        full_weights[0],
        full_weights[1],
        full_weights[2],
        full_weights[3],
        full_weights[4],
        full_weights[5],
        full_weights[6],
    )
    pulled = pullback(cotangent[0])
    ext_grad = pulled[0]
    returned = padded_2(
        ext_grad[atom_count:].astype(jnp.bfloat16), (("graph", 0),), ghost_count
    ).astype(jnp.float32)
    collected = jnp.concatenate(
        [ext_grad[:atom_count], jnp.zeros((1, row_width), jnp.float32)], axis=0
    )
    collected = collected.at[send_left[0]].add(returned[:ghost_count])
    collected = collected.at[send_right[0]].add(returned[3 * ghost_count :])
    grad_features = collected[:atom_count][None]
    grad_terms = tuple((term.astype(jnp.float32) for term in pulled[1:]))
    shard_refs = (w_zero, w_one_re, w_one_im, w_two_re, w_two_im, w_target, alpha_vec)
    grand_totals = lax.psum(grad_terms, ("dp", "graph"))
    position = lax.axis_index("graph")
    shards = tuple(
        (
            lax.dynamic_slice_in_dim(
                summed_all, position * shard_ref.shape[0], shard_ref.shape[0], 0
            )
            for summed_all, shard_ref in zip(grand_totals, shard_refs)
        )
    )
    attended = summed.astype(jnp.bfloat16)[None]
    return (
        attended,
        grad_features,
        shards[0],
        shards[1],
        shards[2],
        shards[3],
        shards[4],
        shards[5],
        shards[6],
    )


def solution(mesh):
    in_specs = (
        P("dp", "graph", None),
        P("dp", "graph", None),
        P("dp", None, "graph"),
        P("dp", "graph"),
        P("dp", "graph"),
        P("dp", "graph"),
        P("dp", "graph"),
        P("graph", None),
        P("graph", None),
        P("graph", None),
        P("graph", None),
        P("graph", None),
        P("graph", None),
        P("graph", None),
    )
    out_specs = (
        P("dp", "graph", None),
        P("dp", "graph", None),
        P("graph", None),
        P("graph", None),
        P("graph", None),
        P("graph", None),
        P("graph", None),
        P("graph", None),
        P("graph", None),
    )
    return jax.shard_map(body, mesh=mesh, in_specs=in_specs, out_specs=out_specs, check_vma=False)
```

profile of v0, /device:TPU:0, one launch (start us, length us, event | category | flops | bytes accessed | tf_op | source)
XLA Modules:
  0.0 474.5 jit_solution(5100000157046764141)
XLA Ops:
  11.7 3.4 collective-permute-start.1
  25.2 9.0 %all_gather.23 = bf16[64,8]{1,0:T(8,128)(2,1)S(1)} all-gather(bf16[8,8]{1,0:T(8,128)(2,1)S(1)} %copy-done.539), channel_id=1, replica_groups=mesh['dp'=4,'graph'=8] {'graph'}, dimensions={0}, use_global_device_ids=true | all-gather | bytes 1152 | tf_op jit(solution)/shard_map/all_gather | solution.py:183
  35.0 8.3 %all_gather.22 = bf16[128,512]{1,0:T(8,128)(2,1)S(1)} all-gather(bf16[16,512]{1,0:T(8,128)(2,1)S(1)} %copy-done.528), channel_id=1, replica_groups=mesh['dp'=4,'graph'=8] {'graph'}, dimensions={0}, use_global_device_ids=true | all-gather | bytes 147456 | tf_op jit(solution)/shard_map/all_gather | solution.py:182
  43.4 10.1 %all_gather.26 = bf16[384,192]{1,0:T(8,128)(2,1)} all-gather(bf16[48,192]{1,0:T(8,128)(2,1)S(1)} %copy-done.524), channel_id=1, replica_groups=mesh['dp'=4,'graph'=8] {'graph'}, dimensions={0}, use_global_device_ids=true | all-gather | bytes 165888 | tf_op jit(solution)/shard_map/all_gather | solution.py:180
  53.5 8.4 %all_gather.27 = bf16[384,192]{1,0:T(8,128)(2,1)S(1)} all-gather(bf16[48,192]{1,0:T(8,128)(2,1)S(1)} %copy-done.525), channel_id=1, replica_groups=mesh['dp'=4,'graph'=8] {'graph'}, dimensions={0}, use_global_device_ids=true | all-gather | bytes 165888 | tf_op jit(solution)/shard_map/all_gather | solution.py:181
  61.8 10.2 %all_gather.24 = bf16[512,256]{1,0:T(8,128)(2,1)} all-gather(bf16[64,256]{1,0:T(8,128)(2,1)S(1)} %copy-done.190), channel_id=1, replica_groups=mesh['dp'=4,'graph'=8] {'graph'}, dimensions={0}, use_global_device_ids=true | all-gather | bytes 294912 | tf_op jit(solution)/shard_map/all_gather | solution.py:178
  72.0 9.5 %all_gather.25 = bf16[512,256]{1,0:T(8,128)(2,1)} all-gather(bf16[64,256]{1,0:T(8,128)(2,1)S(1)} %copy-done.191), channel_id=1, replica_groups=mesh['dp'=4,'graph'=8] {'graph'}, dimensions={0}, use_global_device_ids=true | all-gather | bytes 294912 | tf_op jit(solution)/shard_map/all_gather | solution.py:179
  86.0 1.8 gather_fusion.5
  102.8 2.0 gather_fusion.4
  105.1 1.7 copy_select_fusion
  125.8 1.8 fusion.145
  145.5 2.6 scatter_custom_fusion.1
  152.7 2.3 fusion.126
  155.0 1.8 reshape.3774
  156.8 2.3 fusion.127
  167.0 2.0 fusion.11
  169.0 1.9 fusion.9
  180.4 1.9 slice_multiply_fusion.116
  185.7 1.9 slice_multiply_fusion.49
  195.1 1.9 slice_multiply_fusion.30
  198.4 1.9 fusion.2
  203.6 40.3 %psum.55 = f32[64,8]{1,0:T(8,128)} all-reduce(f32[64,8]{1,0:T(8,128)S(1)} %convert_bitcast_fusion), channel_id=1, replica_groups=mesh['dp'=4,'graph'=8] {'dp','graph'}, use_global_device_ids=true, to_apply=%region_30.32 | all-reduce | flops 512 | bytes 4096 | tf_op jit(solution)/shard_map/psum | solution.py:228
  245.1 2.1 scatter_custom_fusion.6
  247.3 2.0 fusion.7
  267.3 2.0 pad_add_fusion
  271.0 1.9 pad_add_fusion.4
  274.1 13.1 %scatter_fusion.3 = f32[32,3,128]{2,1,0:T(4,128)S(1)} fusion(f32[32,3,128]{2,1,0:T(4,128)S(1)} %broadcast_in_dim.136, s32[192]{0:T(256)S(1)} %bitcast.473, f32[192,3,128]{2,1,0:T(4,128)} %copy.207), kind=kCustom, calls=%fused_computation.14 | custom fusion | flops 73728 | bytes 885504 | tf_op jit(solution)/shard_map/transpose(jvp(jit(_take)))/scatter-add | solution.py:85
  287.3 7.6 %scatter_fusion = f32[32,9,128]{2,1,0:T(8,128)S(1)} fusion(f32[32,9,128]{2,1,0:T(8,128)S(1)} %broadcast_in_dim.133, s32[192]{0:T(256)S(1)} %bitcast.474, f32[192,9,128]{2,1,0:T(8,128)S(1)} %copy.191), kind=kCustom, calls=%fused_computation.11 | custom fusion | flops 221184 | bytes 2654976 | tf_op jit(solution)/shard_map/transpose(jvp(jit(_take)))/scatter-add | solution.py:85
  294.9 7.2 %scatter_fusion.1 = f32[32,7,128]{2,1,0:T(8,128)S(1)} fusion(f32[32,7,128]{2,1,0:T(8,128)S(1)} %broadcast_in_dim.134, s32[192]{0:T(256)S(1)} %bitcast.475, f32[192,7,128]{2,1,0:T(8,128)S(1)} %copy.197), kind=kCustom, calls=%fused_computation.12 | custom fusion | flops 172032 | bytes 2065152 | tf_op jit(solution)/shard_map/transpose(jvp(jit(_take)))/scatter-add | solution.py:85
  302.2 7.2 %scatter_fusion.2 = f32[32,5,128]{2,1,0:T(8,128)S(1)} fusion(f32[32,5,128]{2,1,0:T(8,128)S(1)} %broadcast_in_dim.135, s32[192]{0:T(256)S(1)} %bitcast.476, f32[192,5,128]{2,1,0:T(8,128)S(1)} %copy.203), kind=kCustom, calls=%fused_computation.13 | custom fusion | flops 122880 | bytes 1475328 | tf_op jit(solution)/shard_map/transpose(jvp(jit(_take)))/scatter-add | solution.py:85
  309.9 2.6 collective-permute-start.3
  317.6 140.6 %all-reduce.276.cloned.1.call-done = (f32[640,832]{1,0:T(8,128)}, f32[512,256]{1,0:T(8,128)}, f32[512,256]{1,0:T(8,128)}, f32[384,192]{1,0:T(8,128)}, f32[384,192]{1,0:T(8,128)}, /*index=5*/f32[128,512]{0,1:T(8,128)}) async-done(((f32[640,832]{1,0:T(8,128)}, f32[512,256]{1,0:T(8,128)}, f32[512,256]{1,0:T(8,128)}, f32[384,192]{1,0:T(8,128)}, f32[384,192]{1,0:T(8,128)}, /*index=5*/f32[128,512]{0,1:T(8,128)}), ...) | async-done | bytes 4030480 | tf_op jit(solution)/shard_map/psum | solution.py:228
  (1341 shorter events, 139.0 us)
Async XLA Ops:
  7.2 74.5 %copy-start = (f32[1,16,1600]{2,1,0:T(8,128)S(1)}, f32[1,16,1600]{2,1,0:T(8,128)}, u32[]{:S(2)}) copy-start(f32[1,16,1600]{2,1,0:T(8,128)} %param.17) | copy-start | bytes 307204
  7.2 118.5 %all-gather.2.cloned.1.call-start = ((), (), s32[]{:S(2)}) async-start(), calls=%async_computation | async-start | bytes 1290240 | tf_op jit(solution)/shard_map/all_gather | solution.py:177
  8.0 450.2 %all-reduce.276.cloned.1.call-start = ((), (), s32[]{:S(2)}) async-start(), calls=%async_computation.1 | async-start | bytes 8781824 | tf_op jit(solution)/shard_map/psum | solution.py:228
  11.0 32.4 %copy-start.524 = (bf16[48,192]{1,0:T(8,128)(2,1)S(1)}, bf16[48,192]{1,0:T(8,128)(2,1)}, u32[]{:S(2)}) copy-start(bf16[48,192]{1,0:T(8,128)(2,1)} %param.26) | copy-start | bytes 55300
  11.7 80.4 %collective-permute-start.1 = (f32[8,3200]{1,0:T(8,128)}, f32[8,3200]{1,0:T(8,128)}, u32[]{:S(2)}, u32[]{:S(2)}) collective-permute-start(f32[8,3200]{1,0:T(8,128)} %broadcast_select_fusion), channel_id=1, source_target_pairs={{1,0},{2,1},{3,2},{4,3},{5,4},{6,5},{7,6},{0,7},{9,8},{10,9},{11,1... | collective-permute-start | bytes 307208 | tf_op jit(solution)/shard_map/ppermute | solution.py:17
  15.1 38.4 %copy-start.525 = (bf16[48,192]{1,0:T(8,128)(2,1)S(1)}, bf16[48,192]{1,0:T(8,128)(2,1)}, u32[]{:S(2)}) copy-start(bf16[48,192]{1,0:T(8,128)(2,1)} %param.27) | copy-start | bytes 55300
  15.1 46.8 %copy-start.190 = (bf16[64,256]{1,0:T(8,128)(2,1)S(1)}, bf16[64,256]{1,0:T(8,128)(2,1)}, u32[]{:S(2)}) copy-start(bf16[64,256]{1,0:T(8,128)(2,1)} %param.24) | copy-start | bytes 98308
  15.7 56.3 %copy-start.191 = (bf16[64,256]{1,0:T(8,128)(2,1)S(1)}, bf16[64,256]{1,0:T(8,128)(2,1)}, u32[]{:S(2)}) copy-start(bf16[64,256]{1,0:T(8,128)(2,1)} %param.25) | copy-start | bytes 98308
  16.4 75.7 %collective-permute-start = (f32[8,3200]{1,0:T(8,128)}, f32[8,3200]{1,0:T(8,128)}, u32[]{:S(2)}, u32[]{:S(2)}) collective-permute-start(f32[8,3200]{1,0:T(8,128)} %broadcast_select_fusion.1), channel_id=1, source_target_pairs={{0,1},{1,2},{2,3},{3,4},{4,5},{5,6},{6,7},{7,0},{8,9},{9,10},{10,1... | collective-permute-start | bytes 307208 | tf_op jit(solution)/shard_map/ppermute | solution.py:14
  18.3 80.3 %copy-start.195 = (f32[1,1,192]{2,1,0:T(1,128)}, f32[1,1,192]{2,1,0:T(1,128)S(1)}, u32[]{:S(2)}) copy-start(f32[1,1,192]{2,1,0:T(1,128)S(1)} %get-tuple-element.450) | copy-start | bytes 2308
  18.3 80.3 %copy-start.201 = (f32[1,1,192]{2,1,0:T(1,128)}, f32[1,1,192]{2,1,0:T(1,128)S(1)}, u32[]{:S(2)}) copy-start(f32[1,1,192]{2,1,0:T(1,128)S(1)} %get-tuple-element.451) | copy-start | bytes 2308
  18.3 80.3 %copy-start.207 = (f32[1,1,192]{2,1,0:T(1,128)}, f32[1,1,192]{2,1,0:T(1,128)S(1)}, u32[]{:S(2)}) copy-start(f32[1,1,192]{2,1,0:T(1,128)S(1)} %get-tuple-element.452) | copy-start | bytes 2308
  18.3 97.8 %copy-start.192 = (f32[1,1,192]{2,1,0:T(1,128)}, f32[1,1,192]{2,1,0:T(1,128)S(1)}, u32[]{:S(2)}) copy-start(f32[1,1,192]{2,1,0:T(1,128)S(1)} %get-tuple-element.455) | copy-start | bytes 2308
  18.3 97.8 %copy-start.198 = (f32[1,1,192]{2,1,0:T(1,128)}, f32[1,1,192]{2,1,0:T(1,128)S(1)}, u32[]{:S(2)}) copy-start(f32[1,1,192]{2,1,0:T(1,128)S(1)} %get-tuple-element.456) | copy-start | bytes 2308
  18.4 97.8 %copy-start.204 = (f32[1,1,192]{2,1,0:T(1,128)}, f32[1,1,192]{2,1,0:T(1,128)S(1)}, u32[]{:S(2)}) copy-start(f32[1,1,192]{2,1,0:T(1,128)S(1)} %get-tuple-element.457) | copy-start | bytes 2308
  23.3 68.8 %copy-start.188 = (s32[192,1]{0,1:T(1,128)}, s32[192,1]{0,1:T(1,128)S(1)}, u32[]{:S(2)}) copy-start(s32[192,1]{0,1:T(1,128)S(1)} %get-tuple-element.472) | copy-start | bytes 2308
  43.2 38.4 %copy-start.23 = (bf16[128,512]{1,0:T(8,128)(2,1)}, bf16[128,512]{1,0:T(8,128)(2,1)S(1)}, u32[]{:S(2)}) copy-start(bf16[128,512]{1,0:T(8,128)(2,1)S(1)} %all_gather.22) | copy-start | bytes 393220
  202.7 41.2 %copy-start.163 = (bf16[192,4,64]{0,2,1:T(8,128)(2,1)S(1)}, bf16[192,4,64]{0,2,1:T(8,128)(2,1)}, u32[]{:S(2)}) copy-start(bf16[192,4,64]{0,2,1:T(8,128)(2,1)} %get-tuple-element.64) | copy-start | bytes 294916
  202.7 41.2 %copy-start.169 = (bf16[192,1,128]{2,0,1:T(8,128)(2,1)S(1)}, bf16[192,1,128]{2,0,1:T(8,128)(2,1)}, u32[]{:S(2)}) copy-start(bf16[192,1,128]{2,0,1:T(8,128)(2,1)} %multiply_add_fusion.11) | copy-start | bytes 147460
  202.7 41.2 %copy-start.174 = (bf16[192,1,128]{2,0,1:T(8,128)(2,1)S(1)}, bf16[192,1,128]{2,0,1:T(8,128)(2,1)}, u32[]{:S(2)}) copy-start(bf16[192,1,128]{2,0,1:T(8,128)(2,1)} %multiply_add_fusion.12) | copy-start | bytes 147460
  202.7 41.2 %copy-start.179 = (bf16[192,1,128]{2,0,1:T(8,128)(2,1)S(1)}, bf16[192,1,128]{2,0,1:T(8,128)(2,1)}, u32[]{:S(2)}) copy-start(bf16[192,1,128]{2,0,1:T(8,128)(2,1)} %multiply_add_fusion.13) | copy-start | bytes 147460
  202.7 41.2 %copy-start.184 = (bf16[192,1,128]{2,0,1:T(8,128)(2,1)S(1)}, bf16[192,1,128]{2,0,1:T(8,128)(2,1)}, u32[]{:S(2)}) copy-start(bf16[192,1,128]{2,0,1:T(8,128)(2,1)} %copy-done.183) | copy-start | bytes 147460
  202.7 42.2 %copy-start.50 = (f32[192,1,128]{0,2,1:T(8,128)S(1)}, f32[192,1,128]{0,2,1:T(8,128)}, u32[]{:S(2)}) copy-start(f32[192,1,128]{0,2,1:T(8,128)} %get-tuple-element.185) | copy-start | bytes 294916
  202.7 42.3 %copy-start.49 = (f32[192,1,128]{0,2,1:T(8,128)S(1)}, f32[192,1,128]{0,2,1:T(8,128)}, u32[]{:S(2)}) copy-start(f32[192,1,128]{0,2,1:T(8,128)} %get-tuple-element.188) | copy-start | bytes 294916
  202.7 44.4 %copy-start.172 = (bf16[192,1,128]{2,0,1:T(8,128)(2,1)S(1)}, bf16[192,1,128]{2,0,1:T(8,128)(2,1)}, u32[]{:S(2)}) copy-start(bf16[192,1,128]{2,0,1:T(8,128)(2,1)} %multiply_add_fusion.7) | copy-start | bytes 147460
  202.7 44.4 %copy-start.177 = (bf16[192,1,128]{2,0,1:T(8,128)(2,1)S(1)}, bf16[192,1,128]{2,0,1:T(8,128)(2,1)}, u32[]{:S(2)}) copy-start(bf16[192,1,128]{2,0,1:T(8,128)(2,1)} %multiply_add_fusion.8) | copy-start | bytes 147460
  202.7 44.4 %copy-start.182 = (bf16[192,1,128]{2,0,1:T(8,128)(2,1)S(1)}, bf16[192,1,128]{2,0,1:T(8,128)(2,1)}, u32[]{:S(2)}) copy-start(bf16[192,1,128]{2,0,1:T(8,128)(2,1)} %multiply_add_fusion.9) | copy-start | bytes 147460
  202.7 44.4 %copy-start.187 = (bf16[192,1,128]{2,0,1:T(8,128)(2,1)S(1)}, bf16[192,1,128]{2,0,1:T(8,128)(2,1)}, u32[]{:S(2)}) copy-start(bf16[192,1,128]{2,0,1:T(8,128)(2,1)} %copy-done.185) | copy-start | bytes 147460
  203.4 45.9 %copy-start.545 = (bf16[512,256]{1,0:T(8,128)(2,1)S(1)}, bf16[512,256]{1,0:T(8,128)(2,1)}, u32[]{:S(2)}) copy-start(bf16[512,256]{1,0:T(8,128)(2,1)} %convolution_convert_fusion.5) | copy-start | bytes 786436
  309.8 5.1 %collective-permute-start.2 = (bf16[8,3200]{1,0:T(8,128)(2,1)S(1)}, bf16[8,3200]{1,0:T(8,128)(2,1)S(1)}, u32[]{:S(2)}, u32[]{:S(2)}) collective-permute-start(bf16[8,3200]{1,0:T(8,128)(2,1)S(1)} %get-tuple-element.340), channel_id=1, source_target_pairs={{0,1},{1,2},{2,3},{3,4},{4,5},{5,6},{6,7},{7,0},{8,9},{9,10},{10,1... | collective-permute-start | bytes 153608 | tf_op jit(solution)/shard_map/ppermute | solution.py:14
  309.9 5.0 %collective-permute-start.3 = (bf16[8,3200]{1,0:T(8,128)(2,1)S(1)}, bf16[8,3200]{1,0:T(8,128)(2,1)S(1)}, u32[]{:S(2)}, u32[]{:S(2)}) collective-permute-start(bf16[8,3200]{1,0:T(8,128)(2,1)S(1)} %get-tuple-element.341), channel_id=1, source_target_pairs={{1,0},{2,1},{3,2},{4,3},{5,4},{6,5},{7,6},{0,7},{9,8},{10,9},{11,1... | collective-permute-start | bytes 153608 | tf_op jit(solution)/shard_map/ppermute | solution.py:17
  314.9 152.6 %copy-start.1 = (f32[1,16,1600]{2,1,0:T(8,128)S(1)}, f32[1,16,1600]{2,1,0:T(8,128)}, u32[]{:S(2)}) copy-start(f32[1,16,1600]{2,1,0:T(8,128)} %param.17) | copy-start | bytes 307204
  (520 other events, 1957.1 us)
Sparse Core Ops, SparseCore 0:
  9.9 26.5 all-gather.1
  312.7 145.4 all-reduce.275
where the time goes:
time: 482 us; the launch traced here: 475 us
  waiting for transfers between devices  141 us (29%)
  other arithmetic  119 us (25%)
  blocking collectives  95.7 us (20%)
  local copies, waits for them, and re-layouts  58.4 us (12%)
  matrix products  31.6 us (7%)
  between operations  22.2 us (5%)
  starting transfers between devices  6.1 us (1%)
    psum x1, waiting for transfers between devices, body(): grand_totals = lax.psum(grad_terms, ('dp', 'graph'))  141 us
    psum x1, blocking collectives, body(): grand_totals = lax.psum(grad_terms, ('dp', 'graph'))  40.3 us
    scatter-add x4, other arithmetic, attend(): jnp.take(coeffs[:, degree * degree:(degree + 1) * (degree + 1), :], edge_...  35.1 us
    mul x13, other arithmetic, apply_block(): total = total + block[row, column][:, None] * source_part[:, column, :]  17.5 us
    unnamed x26, other arithmetic  15.7 us
    all_gather x1, blocking collectives, body(): lax.all_gather(w_one_re, 'graph', axis=0, tiled=True)  10.2 us
    all_gather x1, blocking collectives, body(): lax.all_gather(w_two_re, 'graph', axis=0, tiled=True)  10.1 us
    dynamic_slice x7, local copies, waits for them, and re-layouts, body(): lax.dynamic_slice_in_dim(summed_all, position * shard_ref.shape[0], shard...  9.83 us
  transfers between devices with their start and end apart: 6, of which 1 were waited for; matrix products, arithmetic and copies ran while one was open for 12% of the time, Pallas kernels for 0%

commit v1 on v0

--- a/solution.py
+++ b/solution.py
@@ -225,7 +225,7 @@
     grad_features = collected[:atom_count][None]
     grad_terms = tuple((term.astype(jnp.float32) for term in pulled[1:]))
     shard_refs = (w_zero, w_one_re, w_one_im, w_two_re, w_two_im, w_target, alpha_vec)
-    grand_totals = lax.psum(grad_terms, ("dp", "graph"))
+    grand_totals = lax.psum(lax.psum(grad_terms, "graph"), "dp")
     position = lax.axis_index("graph")
     shards = tuple(
         (

time: 482 us -> 535 us (1.11)
  waiting for transfers between devices: 141 us -> 195 us
    psum x1 -> x2, waiting for transfers between devices: 141 us -> 195 us  [body(): grand_totals = lax.psum(lax.psum(grad_terms, 'graph'), 'dp')]
    psum x1 -> x2, blocking collectives: 40.3 us -> 44 us  [body(): grand_totals = lax.psum(lax.psum(grad_terms, 'graph'), 'dp')]
    unnamed x1103 -> x1171, local copies, waits for them, and re-layouts: 9.68 us -> 11.4 us
  transfers between devices with their start and end apart: 6 -> 7, of which waited for: 1 -> 2; matrix products, arithmetic and copies ran while one was open for 12% -> 12% of each run, Pallas kernels for 0% -> 0%
where the time goes in v1:
time: 535 us; the launch traced here: 529 us
  waiting for transfers between devices  195 us (36%)
  other arithmetic  119 us (22%)
  blocking collectives  99.5 us (19%)
  local copies, waits for them, and re-layouts  57.4 us (11%)
  matrix products  29 us (5%)
  between operations  22.6 us (4%)
  starting transfers between devices  6.17 us (1%)
    psum x2, waiting for transfers between devices, body(): grand_totals = lax.psum(lax.psum(grad_terms, 'graph'), 'dp')  195 us
    psum x2, blocking collectives, body(): grand_totals = lax.psum(lax.psum(grad_terms, 'graph'), 'dp')  44 us
    scatter-add x4, other arithmetic, attend(): jnp.take(coeffs[:, degree * degree:(degree + 1) * (degree + 1), :], edge_...  36.1 us
    mul x13, other arithmetic, apply_block(): total = total + block[row, column][:, None] * source_part[:, column, :]  17.4 us
    unnamed x1171, local copies, waits for them, and re-layouts  11.4 us
    unnamed x26, other arithmetic  11 us
  transfers between devices with their start and end apart: 7, of which 2 were waited for; matrix products, arithmetic and copies ran while one was open for 12% of the time, Pallas kernels for 0%

profile of v1, /device:TPU:0, one launch (start us, length us, event | category | flops | bytes accessed | tf_op | source)
XLA Modules:
  0.0 528.8 jit_solution(6878452874503521862)
XLA Ops:
  11.7 3.4 collective-permute-start.1
  25.2 9.0 %all_gather.23 = bf16[64,8]{1,0:T(8,128)(2,1)S(1)} all-gather(bf16[8,8]{1,0:T(8,128)(2,1)S(1)} %copy-done.573), channel_id=1, replica_groups=mesh['dp'=4,'graph'=8] {'graph'}, dimensions={0}, use_global_device_ids=true | all-gather | bytes 1152 | tf_op jit(solution)/shard_map/all_gather | solution.py:183
  35.5 8.3 %all_gather.22 = bf16[128,512]{1,0:T(8,128)(2,1)S(1)} all-gather(bf16[16,512]{1,0:T(8,128)(2,1)S(1)} %copy-done.560), channel_id=1, replica_groups=mesh['dp'=4,'graph'=8] {'graph'}, dimensions={0}, use_global_device_ids=true | all-gather | bytes 147456 | tf_op jit(solution)/shard_map/all_gather | solution.py:182
  43.9 10.1 %all_gather.26 = bf16[384,192]{1,0:T(8,128)(2,1)} all-gather(bf16[48,192]{1,0:T(8,128)(2,1)S(1)} %copy-done.556), channel_id=1, replica_groups=mesh['dp'=4,'graph'=8] {'graph'}, dimensions={0}, use_global_device_ids=true | all-gather | bytes 165888 | tf_op jit(solution)/shard_map/all_gather | solution.py:180
  54.0 8.3 %all_gather.27 = bf16[384,192]{1,0:T(8,128)(2,1)S(1)} all-gather(bf16[48,192]{1,0:T(8,128)(2,1)S(1)} %copy-done.557), channel_id=1, replica_groups=mesh['dp'=4,'graph'=8] {'graph'}, dimensions={0}, use_global_device_ids=true | all-gather | bytes 165888 | tf_op jit(solution)/shard_map/all_gather | solution.py:181
  62.4 10.2 %all_gather.24 = bf16[512,256]{1,0:T(8,128)(2,1)} all-gather(bf16[64,256]{1,0:T(8,128)(2,1)S(1)} %copy-done.200), channel_id=1, replica_groups=mesh['dp'=4,'graph'=8] {'graph'}, dimensions={0}, use_global_device_ids=true | all-gather | bytes 294912 | tf_op jit(solution)/shard_map/all_gather | solution.py:178
  72.5 9.6 %all_gather.25 = bf16[512,256]{1,0:T(8,128)(2,1)} all-gather(bf16[64,256]{1,0:T(8,128)(2,1)S(1)} %copy-done.201), channel_id=1, replica_groups=mesh['dp'=4,'graph'=8] {'graph'}, dimensions={0}, use_global_device_ids=true | all-gather | bytes 294912 | tf_op jit(solution)/shard_map/all_gather | solution.py:179
  86.5 1.8 gather_fusion.5
  105.3 2.0 gather_fusion.4
  119.8 1.7 convolution_subtract_fusion.1
  129.6 1.8 fusion.145
  144.2 1.9 multiply_reduce_fusion.10
  162.3 2.1 fusion.11
  164.3 2.0 fusion.9
  175.9 1.9 slice_multiply_fusion.116
  177.9 1.9 slice_multiply_fusion.125
  181.7 1.8 slice_multiply_fusion.49
  190.7 1.8 slice_multiply_fusion.30
  193.9 1.9 fusion.2
  200.2 2.1 scatter_custom_fusion.6
  204.6 2.2 scatter_custom_fusion.1
  218.4 2.0 pad_add_fusion
  222.2 1.9 pad_add_fusion.4
  227.0 7.2 %scatter_fusion.3 = f32[32,3,128]{2,1,0:T(4,128)S(1)} fusion(f32[32,3,128]{2,1,0:T(4,128)S(1)} %broadcast_in_dim.136, s32[192]{0:T(256)S(1)} %bitcast.473, f32[192,3,128]{2,1,0:T(4,128)S(1)} %copy.207), kind=kCustom, calls=%fused_computation.14 | custom fusion | flops 73728 | bytes 885504 | tf_op jit(solution)/shard_map/transpose(jvp(jit(_take)))/scatter-add | solution.py:85
  234.2 7.6 %scatter_fusion = f32[32,9,128]{2,1,0:T(8,128)S(1)} fusion(f32[32,9,128]{2,1,0:T(8,128)S(1)} %broadcast_in_dim.133, s32[192]{0:T(256)S(1)} %bitcast.474, f32[192,9,128]{2,1,0:T(8,128)S(1)} %copy.191), kind=kCustom, calls=%fused_computation.11 | custom fusion | flops 221184 | bytes 2654976 | tf_op jit(solution)/shard_map/transpose(jvp(jit(_take)))/scatter-add | solution.py:85
  241.9 14.0 %scatter_fusion.1 = f32[32,7,128]{2,1,0:T(8,128)S(1)} fusion(f32[32,7,128]{2,1,0:T(8,128)S(1)} %broadcast_in_dim.134, s32[192]{0:T(256)S(1)} %bitcast.475, f32[192,7,128]{2,1,0:T(8,128)} %copy.197), kind=kCustom, calls=%fused_computation.12 | custom fusion | flops 172032 | bytes 2065152 | tf_op jit(solution)/shard_map/transpose(jvp(jit(_take)))/scatter-add | solution.py:85
  256.0 7.2 %scatter_fusion.2 = f32[32,5,128]{2,1,0:T(8,128)S(1)} fusion(f32[32,5,128]{2,1,0:T(8,128)S(1)} %broadcast_in_dim.135, s32[192]{0:T(256)S(1)} %bitcast.476, f32[192,5,128]{2,1,0:T(8,128)S(1)} %copy-done.4), kind=kCustom, calls=%fused_computation.13 | custom fusion | flops 122880 | bytes 1475328 | tf_op jit(solution)/shard_map/transpose(jvp(jit(_take)))/scatter-add | solution.py:85
  264.6 82.6 %all-reduce.278.cloned.1.call-done = (f32[640,832]{1,0:T(8,128)}, f32[512,256]{1,0:T(8,128)}, f32[512,256]{1,0:T(8,128)}, f32[384,192]{1,0:T(8,128)}, f32[384,192]{1,0:T(8,128)}, /*index=5*/f32[128,512]{0,1:T(8,128)}) async-done(((f32[640,832]{1,0:T(8,128)}, f32[512,256]{1,0:T(8,128)}, f32[512,256]{1,0:T(8,128)}, f32[384,192]{1,0:T(8,128)}, f32[384,192]{1,0:T(8,128)}, /*index=5*/f32[128,512]{0,1:T(8,128)}), ...) | async-done | bytes 4030480 | tf_op jit(solution)/shard_map/psum | solution.py:228
  348.3 2.6 collective-permute-start.3
  350.9 23.5 %psum.110 = f32[64,8]{1,0:T(8,128)S(1)} all-reduce(f32[64,8]{1,0:T(8,128)S(1)} %convert_bitcast_fusion), channel_id=1, replica_groups=mesh['dp'=4,'graph'=8] {'graph'}, use_global_device_ids=true, to_apply=%region_36.38 | all-reduce | flops 512 | bytes 4096 | tf_op jit(solution)/shard_map/psum | solution.py:228
  374.4 20.5 %psum.111 = f32[64,8]{1,0:T(8,128)S(1)} all-reduce(f32[64,8]{1,0:T(8,128)S(1)} %psum.110), channel_id=1, replica_groups=mesh['dp'=4,'graph'=8] {'dp'}, use_global_device_ids=true, to_apply=%region_37.39 | all-reduce | flops 512 | bytes 4096 | tf_op jit(solution)/shard_map/psum | solution.py:228
  400.7 112.1 %all-reduce.280.cloned.1.call-done = (f32[640,832]{1,0:T(8,128)}, f32[512,256]{1,0:T(8,128)}, f32[512,256]{1,0:T(8,128)}, f32[384,192]{1,0:T(8,128)}, f32[384,192]{1,0:T(8,128)}, /*index=5*/f32[128,512]{0,1:T(8,128)}) async-done(((f32[640,832]{1,0:T(8,128)}, f32[512,256]{1,0:T(8,128)}, f32[512,256]{1,0:T(8,128)}, f32[384,192]{1,0:T(8,128)}, f32[384,192]{1,0:T(8,128)}, /*index=5*/f32[128,512]{0,1:T(8,128)}), ...) | async-done | bytes 4030480 | tf_op jit(solution)/shard_map/psum | solution.py:228
  (1413 shorter events, 138.9 us)
Async XLA Ops:
  7.2 75.1 %copy-start = (f32[1,16,1600]{2,1,0:T(8,128)S(1)}, f32[1,16,1600]{2,1,0:T(8,128)}, u32[]{:S(2)}) copy-start(f32[1,16,1600]{2,1,0:T(8,128)} %param.17) | copy-start | bytes 307204
  7.2 122.4 %all-gather.2.cloned.1.call-start = ((), (), s32[]{:S(2)}) async-start(), calls=%async_computation | async-start | bytes 1290240 | tf_op jit(solution)/shard_map/all_gather | solution.py:177
  8.0 339.3 %all-reduce.278.cloned.1.call-start = ((), (), s32[]{:S(2)}) async-start(), calls=%async_computation.1 | async-start | bytes 8781824 | tf_op jit(solution)/shard_map/psum | solution.py:228
  11.7 81.6 %collective-permute-start.1 = (f32[8,3200]{1,0:T(8,128)}, f32[8,3200]{1,0:T(8,128)}, u32[]{:S(2)}, u32[]{:S(2)}) collective-permute-start(f32[8,3200]{1,0:T(8,128)} %broadcast_select_fusion), channel_id=1, source_target_pairs={{1,0},{2,1},{3,2},{4,3},{5,4},{6,5},{7,6},{0,7},{9,8},{10,9},{11,1... | collective-permute-start | bytes 307208 | tf_op jit(solution)/shard_map/ppermute | solution.py:17
  15.7 56.8 %copy-start.201 = (bf16[64,256]{1,0:T(8,128)(2,1)S(1)}, bf16[64,256]{1,0:T(8,128)(2,1)}, u32[]{:S(2)}) copy-start(bf16[64,256]{1,0:T(8,128)(2,1)} %param.25) | copy-start | bytes 98308
  16.4 76.9 %collective-permute-start = (f32[8,3200]{1,0:T(8,128)}, f32[8,3200]{1,0:T(8,128)}, u32[]{:S(2)}, u32[]{:S(2)}) collective-permute-start(f32[8,3200]{1,0:T(8,128)} %broadcast_select_fusion.1), channel_id=1, source_target_pairs={{0,1},{1,2},{2,3},{3,4},{4,5},{5,6},{6,7},{7,0},{8,9},{9,10},{10,1... | collective-permute-start | bytes 307208 | tf_op jit(solution)/shard_map/ppermute | solution.py:14
  18.4 98.3 %copy-start.204 = (f32[1,1,192]{2,1,0:T(1,128)}, f32[1,1,192]{2,1,0:T(1,128)S(1)}, u32[]{:S(2)}) copy-start(f32[1,1,192]{2,1,0:T(1,128)S(1)} %get-tuple-element.461) | copy-start | bytes 2308
  19.0 64.2 %copy-start.241 = (f32[1,1,192]{2,1,0:T(1,128)}, f32[1,1,192]{2,1,0:T(1,128)S(1)}, u32[]{:S(2)}) copy-start(f32[1,1,192]{2,1,0:T(1,128)S(1)} %get-tuple-element.430) | copy-start | bytes 2308
  19.0 64.5 %copy-start.229 = (f32[1,1,192]{2,1,0:T(1,128)}, f32[1,1,192]{2,1,0:T(1,128)S(1)}, u32[]{:S(2)}) copy-start(f32[1,1,192]{2,1,0:T(1,128)S(1)} %get-tuple-element.429) | copy-start | bytes 2308
  19.1 66.1 %copy-start.253 = (f32[1,1,192]{2,1,0:T(1,128)}, f32[1,1,192]{2,1,0:T(1,128)S(1)}, u32[]{:S(2)}) copy-start(f32[1,1,192]{2,1,0:T(1,128)S(1)} %get-tuple-element.431) | copy-start | bytes 2308
  19.1 66.1 %copy-start.258 = (f32[1,1,192]{2,1,0:T(1,128)}, f32[1,1,192]{2,1,0:T(1,128)S(1)}, u32[]{:S(2)}) copy-start(f32[1,1,192]{2,1,0:T(1,128)S(1)} %get-tuple-element.432) | copy-start | bytes 2308
  19.1 66.1 %copy-start.263 = (f32[1,1,192]{2,1,0:T(1,128)}, f32[1,1,192]{2,1,0:T(1,128)S(1)}, u32[]{:S(2)}) copy-start(f32[1,1,192]{2,1,0:T(1,128)S(1)} %get-tuple-element.433) | copy-start | bytes 2308
  19.1 66.1 %copy-start.219 = (f32[1,1,192]{2,1,0:T(1,128)}, f32[1,1,192]{2,1,0:T(1,128)S(1)}, u32[]{:S(2)}) copy-start(f32[1,1,192]{2,1,0:T(1,128)S(1)} %get-tuple-element.428) | copy-start | bytes 2308
  20.5 62.7 %copy-start.293 = (f32[1,1,192]{2,1,0:T(1,128)}, f32[1,1,192]{2,1,0:T(1,128)S(1)}, u32[]{:S(2)}) copy-start(f32[1,1,192]{2,1,0:T(1,128)S(1)} %get-tuple-element.411) | copy-start | bytes 2308
  20.5 62.7 %copy-start.305 = (f32[1,1,192]{2,1,0:T(1,128)}, f32[1,1,192]{2,1,0:T(1,128)S(1)}, u32[]{:S(2)}) copy-start(f32[1,1,192]{2,1,0:T(1,128)S(1)} %get-tuple-element.412) | copy-start | bytes 2308
  20.6 62.7 %copy-start.321 = (f32[1,1,192]{2,1,0:T(1,128)}, f32[1,1,192]{2,1,0:T(1,128)S(1)}, u32[]{:S(2)}) copy-start(f32[1,1,192]{2,1,0:T(1,128)S(1)} %get-tuple-element.413) | copy-start | bytes 2308
  23.3 59.4 %copy-start.572 = (s32[192,1]{0,1:T(1,128)}, s32[192,1]{0,1:T(1,128)S(1)}, u32[]{:S(2)}) copy-start(s32[192,1]{0,1:T(1,128)S(1)} %get-tuple-element.477) | copy-start | bytes 2308
  23.3 70.0 %copy-start.198 = (s32[192,1]{0,1:T(1,128)}, s32[192,1]{0,1:T(1,128)S(1)}, u32[]{:S(2)}) copy-start(s32[192,1]{0,1:T(1,128)S(1)} %get-tuple-element.478) | copy-start | bytes 2308
  25.2 58.1 %copy-start.527 = (f32[1,1,192]{2,1,0:T(1,128)}, f32[1,1,192]{2,1,0:T(1,128)S(1)}, u32[]{:S(2)}) copy-start(f32[1,1,192]{2,1,0:T(1,128)S(1)} %get-tuple-element.469) | copy-start | bytes 2308
  25.2 58.2 %copy-start.535 = (f32[1,1,192]{2,1,0:T(1,128)}, f32[1,1,192]{2,1,0:T(1,128)S(1)}, u32[]{:S(2)}) copy-start(f32[1,1,192]{2,1,0:T(1,128)S(1)} %get-tuple-element.470) | copy-start | bytes 2308
  25.2 58.2 %copy-start.545 = (f32[1,1,192]{2,1,0:T(1,128)}, f32[1,1,192]{2,1,0:T(1,128)S(1)}, u32[]{:S(2)}) copy-start(f32[1,1,192]{2,1,0:T(1,128)S(1)} %get-tuple-element.468) | copy-start | bytes 2308
  25.2 58.2 %copy-start.549 = (f32[1,1,192]{2,1,0:T(1,128)}, f32[1,1,192]{2,1,0:T(1,128)S(1)}, u32[]{:S(2)}) copy-start(f32[1,1,192]{2,1,0:T(1,128)S(1)} %get-tuple-element.471) | copy-start | bytes 2308
  25.2 58.2 %copy-start.553 = (f32[1,1,192]{2,1,0:T(1,128)}, f32[1,1,192]{2,1,0:T(1,128)S(1)}, u32[]{:S(2)}) copy-start(f32[1,1,192]{2,1,0:T(1,128)S(1)} %get-tuple-element.476) | copy-start | bytes 2308
  263.3 249.4 %all-reduce.280.cloned.1.call-start = ((), (), s32[]{:S(2)}) async-start(), calls=%async_computation.2 | async-start | bytes 8781824 | tf_op jit(solution)/shard_map/psum | solution.py:228
  347.4 48.5 %copy-start.340 = (f32[1,1,192]{2,1,0:T(1,128)S(1)}, f32[1,1,192]{2,1,0:T(1,128)}, u32[]{:S(2)}) copy-start(f32[1,1,192]{2,1,0:T(1,128)} %get-tuple-element.398) | copy-start | bytes 2308
  347.4 48.5 %copy-start.399 = (f32[1,1,192]{2,1,0:T(1,128)S(1)}, f32[1,1,192]{2,1,0:T(1,128)}, u32[]{:S(2)}) copy-start(f32[1,1,192]{2,1,0:T(1,128)} %get-tuple-element.362) | copy-start | bytes 2308
  347.4 48.5 %copy-start.403 = (f32[1,1,192]{2,1,0:T(1,128)S(1)}, f32[1,1,192]{2,1,0:T(1,128)}, u32[]{:S(2)}) copy-start(f32[1,1,192]{2,1,0:T(1,128)} %get-tuple-element.371) | copy-start | bytes 2308
  347.4 48.5 %copy-start.458 = (f32[1,1,192]{2,1,0:T(1,128)S(1)}, f32[1,1,192]{2,1,0:T(1,128)}, u32[]{:S(2)}) copy-start(f32[1,1,192]{2,1,0:T(1,128)} %get-tuple-element.380) | copy-start | bytes 2308
  347.4 48.5 %copy-start.462 = (f32[1,1,192]{2,1,0:T(1,128)S(1)}, f32[1,1,192]{2,1,0:T(1,128)}, u32[]{:S(2)}) copy-start(f32[1,1,192]{2,1,0:T(1,128)} %get-tuple-element.389) | copy-start | bytes 2308
  348.2 49.8 %collective-permute-start.2 = (bf16[8,3200]{1,0:T(8,128)(2,1)S(1)}, bf16[8,3200]{1,0:T(8,128)(2,1)S(1)}, u32[]{:S(2)}, u32[]{:S(2)}) collective-permute-start(bf16[8,3200]{1,0:T(8,128)(2,1)S(1)} %get-tuple-element.346), channel_id=1, source_target_pairs={{0,1},{1,2},{2,3},{3,4},{4,5},{5,6},{6,7},{7,0},{8,9},{9,10},{10,1... | collective-permute-start | bytes 153608 | tf_op jit(solution)/shard_map/ppermute | solution.py:14
  348.3 49.8 %collective-permute-start.3 = (bf16[8,3200]{1,0:T(8,128)(2,1)S(1)}, bf16[8,3200]{1,0:T(8,128)(2,1)S(1)}, u32[]{:S(2)}, u32[]{:S(2)}) collective-permute-start(bf16[8,3200]{1,0:T(8,128)(2,1)S(1)} %get-tuple-element.347), channel_id=1, source_target_pairs={{1,0},{2,1},{3,2},{4,3},{5,4},{6,5},{7,6},{0,7},{9,8},{10,9},{11,1... | collective-permute-start | bytes 153608 | tf_op jit(solution)/shard_map/ppermute | solution.py:17
  398.0 124.0 %copy-start.1 = (f32[1,16,1600]{2,1,0:T(8,128)S(1)}, f32[1,16,1600]{2,1,0:T(8,128)}, u32[]{:S(2)}) copy-start(f32[1,16,1600]{2,1,0:T(8,128)} %param.17) | copy-start | bytes 307204
  (555 other events, 3717.1 us)
Sparse Core Ops, SparseCore 0:
  9.9 26.5 all-gather.1
  263.5 83.7 all-reduce.277
  350.1 162.5 all-reduce.279
